TPU v7x, 512 devices: a whole 4x8x8 slice. The times are simulated.
512 devices in a mesh: grp: 16 (over z, core), blk: 32 (over y, x).
Axes of the slice: x: 4, y: 8, z: 8, core: 2. Of those that a mesh axis runs over, the one named last changes fastest.
Arguments:
- integrals: bfloat16 [32, 2048, 2048], P('blk', None, 'grp'), as said below
- tile_mask: int32 [16, 16], replicated, may hold values from 0 to 1, as said below
- tile_owner: int32 [16], replicated, may hold values from 0 to 15, as said below
- occupied_tiles: bfloat16 [16384, 128], P(('grp', 'blk')), may hold values from -0.1875 to 0.1875
- occupied_offsets: int32 [8], replicated, may hold values from 0 to 15, as said below
- virtual_tiles: bfloat16 [16384, 128], P(('grp', 'blk')), may hold values from -0.1875 to 0.1875
- virtual_offsets: int32 [8], replicated, may hold values from 0 to 15, as said below
Outputs:
- polarizability: float32 [32, 32], P('blk')
Inputs may be any that keep to these rules, and one draw needn't show every extreme that they name: `integrals`: after column slot s is placed at basis tile tile_owner[s], the tensor is symmetric in its two basis indices. `tile_mask`: symmetric, with ones on the diagonal. `tile_owner`: each tile exactly once. `occupied_offsets`: 8 different tile offsets, among them 0 and 15. `virtual_offsets`: 8 different tile offsets, among them 0 and 15.
All inputs are finite; a program needn't handle non-finite values.
Results may differ from a plain program's by a relative error of at most 0.004.
Values may be sent and summed in bfloat16 or wider, within the bound.
A program may use at most 64 MiB of HBM per device.

v0:
```python
import jax
import jax.numpy as jnp
from jax import lax
from jax.sharding import PartitionSpec as P

NT = 16


def body(
    integrals,
    tile_mask,
    tile_owner,
    occupied_tiles,
    occupied_offsets,
    virtual_tiles,
    virtual_offsets,
):
    aux_local, basis_size, local_width = integrals.shape
    tile_width = basis_size // NT
    kcount = occupied_offsets.shape[0]
    local_tiles = local_width // tile_width
    group_index = lax.axis_index("grp")
    local_owner = lax.dynamic_slice_in_dim(tile_owner, group_index * local_tiles, local_tiles)
    matches = (local_owner[None, :, None] == jnp.arange(NT, dtype=jnp.int32)[None, None, :]).astype(
        jnp.int32
    )
    column_mask = jnp.sum(tile_mask[:, None, :] * matches, axis=2)
    blocked = integrals.reshape(aux_local, NT, tile_width, local_tiles, tile_width)
    masked = blocked * column_mask.astype(jnp.bfloat16)[None, :, None, :, None]
    masked = masked.reshape(aux_local, NT, tile_width, local_width)
    occupied_all, virtual_all = (
        lax.all_gather(occupied_tiles, ("grp", "blk"), axis=0, tiled=True),
        lax.all_gather(virtual_tiles, ("grp", "blk"), axis=0, tiled=True),
    )
    occupied_all = occupied_all.reshape(NT, kcount, tile_width, tile_width)
    virtual_all = virtual_all.reshape(NT, kcount, tile_width, tile_width)
    source_rows = (tile_owner[:, None] - occupied_offsets[None, :]) % NT
    partner_rows = (tile_owner[:, None] + virtual_offsets[None, :]) % NT
    virtual_pick = virtual_all[tile_owner]
    occupied_sum = jnp.zeros((aux_local, NT, tile_width, local_width), jnp.float32)
    virtual_sum = jnp.zeros((aux_local, local_width, NT, tile_width), jnp.float32)
    for slot in range(kcount):
        occupied_pick = occupied_all[source_rows[:, slot], slot]
        occupied_inputs = masked[:, source_rows[:, slot]]
        occupied_sum = occupied_sum + jnp.einsum(
            "tmn,ptml->ptnl", occupied_pick, occupied_inputs, preferred_element_type=jnp.float32
        )
        virtual_inputs = masked[:, partner_rows[:, slot]]
        virtual_sum = virtual_sum + jnp.einsum(
            "tnm,ptml->pltn",
            virtual_pick[:, slot],
            virtual_inputs,
            preferred_element_type=jnp.float32,
        )
    occupied_part = occupied_sum.astype(jnp.bfloat16)
    virtual_part = virtual_sum.astype(jnp.bfloat16).reshape(
        aux_local, local_tiles, tile_width, basis_size
    )
    occupied_moved = lax.all_to_all(occupied_part, "grp", split_axis=1, concat_axis=3, tiled=True)
    occupied_full, virtual_full = (
        lax.all_to_all(occupied_moved, "blk", split_axis=2, concat_axis=0, tiled=True),
        lax.all_to_all(virtual_part, "blk", split_axis=2, concat_axis=0, tiled=True),
    )
    left_side = occupied_full.reshape(occupied_full.shape[0], -1)
    right_side = virtual_full.reshape(virtual_full.shape[0], -1)
    partial_sum = jnp.einsum(
        "pe,qe->pq", left_side, right_side, preferred_element_type=jnp.float32
    ) * (1.0 / basis_size)
    total = lax.psum(partial_sum, ("grp", "blk"))
    return lax.dynamic_slice_in_dim(total, lax.axis_index("blk") * aux_local, aux_local, 0)


def solution(mesh):
    in_specs = (
        P("blk", None, "grp"),
        P(),
        P(),
        P(("grp", "blk"), None),
        P(),
        P(("grp", "blk"), None),
        P(),
    )
    out_specs = P("blk", None)
    return jax.shard_map(body, mesh=mesh, in_specs=in_specs, out_specs=out_specs, check_vma=False)
```

profile of v0, /device:TPU:1, one launch (start us, length us, event | category | flops | bytes accessed | tf_op | source)
XLA Modules:
  0.0 427.2 jit_solution(16286854891178512670)
XLA Ops:
  34.0 102.1 %all-gather.3.cloned.1.call-done = bf16[16384,128]{1,0:T(8,128)(2,1)} async-done(((bf16[32,128]{1,0:T(8,128)(2,1)}), bf16[16384,128]{1,0:T(8,128)(2,1)}) %all-gather.3.cloned.1.call-update) | async-done | bytes 4194320 | tf_op jit(solution)/shard_map/all_gather | solution.py:32
  136.1 3.6 gather_fusion.1
  139.7 3.6 gather_fusion.3
  143.3 3.6 gather_fusion.5
  146.9 3.6 gather_fusion.7
  150.5 2.9 gather_fusion.9
  153.4 2.8 gather_fusion.11
  156.2 2.8 gather_fusion.13
  159.1 2.8 gather_fusion.15
  162.0 1.7 fusion.25
  163.7 1.6 convolution_add_fusion.13
  168.3 6.0 %all-to-all-start = ((bf16[1,16,128,128]{2,3,0,1:T(8,128)(2,1)}), bf16[1,16,128,128]{2,3,0,1:T(8,128)(2,1)S(1)}, u32[]{:S(2)}, u32[]{:S(2)}) async-start(bf16[1,16,128,128]{2,3,0,1:T(8,128)(2,1)} %fusion.2), calls=%async_computation | async-start | bytes 1048576 | tf_op jit(solution)/shard_map/all_to_all | solution.py:59
  174.4 81.7 %all-gather.5.cloned.1.call-done = bf16[16384,128]{1,0:T(8,128)(2,1)} async-done(((bf16[32,128]{1,0:T(8,128)(2,1)}), bf16[16384,128]{1,0:T(8,128)(2,1)}) %all-gather.5.cloned.1.call-update) | async-done | bytes 4194320 | tf_op jit(solution)/shard_map/all_gather | solution.py:33
  256.1 5.4 %gather_fusion.17 = bf16[16,8,128,128]{3,2,1,0:T(8,128)(2,1)} fusion(bf16[16,8,128,128]{3,2,1,0:T(8,128)(2,1)} %bitcast.152, s32[1024]{0:T(1024)S(1)} %pad_clamp_fusion.8), kind=kCustom, calls=%fused_computation.17 | custom fusion | bytes 8388672 | tf_op jit(solution)/shard_map/gather | solution.py:39
  262.9 1.6 convolution_add_fusion.6
  268.0 3.7 reduce.6
  272.9 6.9 %all-to-all-start.2 = ((bf16[32,2,4096]{2,1,0:T(2,128)(2,1)}), bf16[32,2,4096]{2,1,0:T(2,128)(2,1)S(1)}, u32[]{:S(2)}, u32[]{:S(2)}) async-start(bf16[32,2,4096]{2,1,0:T(2,128)(2,1)} %reshape.405), calls=%async_computation.2 | async-start | bytes 1048576 | tf_op jit(solution)/shard_map/all_to_all | solution.py:62
  280.7 3.7 reduce.7
  285.6 10.8 %all-to-all-done.2 = bf16[32,2,4096]{2,1,0:T(2,128)(2,1)S(1)} async-done(((bf16[32,2,4096]{2,1,0:T(2,128)(2,1)}), bf16[32,2,4096]{2,1,0:T(2,128)(2,1)S(1)}, u32[]{:S(2)}, u32[]{:S(2)}) %all-to-all-start.2) | async-done | bytes 524320 | tf_op jit(solution)/shard_map/all_to_all | solution.py:62
  296.4 5.2 %all-to-all-start.1 = ((bf16[32,2,4096]{2,1,0:T(2,128)(2,1)}), bf16[32,2,4096]{2,1,0:T(2,128)(2,1)S(1)}, u32[]{:S(2)}, u32[]{:S(2)}) async-start(bf16[32,2,4096]{2,1,0:T(2,128)(2,1)} %reshape.407), calls=%async_computation.1 | async-start | bytes 1048576 | tf_op jit(solution)/shard_map/all_to_all | solution.py:61
  302.2 3.0 bitcast_reduce_fusion.1
  305.4 11.3 %all-to-all-done.1 = bf16[32,2,4096]{2,1,0:T(2,128)(2,1)S(1)} async-done(((bf16[32,2,4096]{2,1,0:T(2,128)(2,1)}), bf16[32,2,4096]{2,1,0:T(2,128)(2,1)S(1)}, u32[]{:S(2)}, u32[]{:S(2)}) %all-to-all-start.1) | async-done | bytes 524320 | tf_op jit(solution)/shard_map/all_to_all | solution.py:61
  317.2 3.0 bitcast_reduce_fusion
  321.6 98.2 %psum.7 = f32[32,32]{1,0:T(8,128)S(1)} all-reduce(f32[32,32]{1,0:T(8,128)S(1)} %fusion.3), channel_id=1, replica_groups=mesh['grp'=16,'blk'=32] {'grp','blk'}, use_global_device_ids=true, to_apply=%region_1.2 | all-reduce | flops 1024 | bytes 8192 | tf_op jit(solution)/shard_map/psum | solution.py:69
  (95 shorter events, 41.7 us)
Async XLA Ops:
  6.5 129.6 %all-gather.3.cloned.1.call-start = ((), (), s32[]{:S(2)}) async-start(), calls=%async_computation.3 | async-start | bytes 4202496 | tf_op jit(solution)/shard_map/all_gather | solution.py:32
  7.3 248.8 %all-gather.5.cloned.1.call-start = ((), (), s32[]{:S(2)}) async-start(), calls=%async_computation.4 | async-start | bytes 4202496 | tf_op jit(solution)/shard_map/all_gather | solution.py:33
  23.3 10.7 %copy-start.15 = (s32[16]{0:T(128)S(1)}, s32[16]{0:T(128)}, u32[]{:S(2)}) copy-start(s32[16]{0:T(128)} %param.9) | copy-start | bytes 196
  161.9 3.4 copy-start.2
  161.9 3.4 copy-start.11
  161.9 3.7 copy-start.1
  161.9 3.7 copy-start.10
  163.7 2.4 copy-start.13
  165.3 1.1 copy-start.12
  165.7 1.1 copy-start.14
  168.3 104.6 %all-to-all-start = ((bf16[1,16,128,128]{2,3,0,1:T(8,128)(2,1)}), bf16[1,16,128,128]{2,3,0,1:T(8,128)(2,1)S(1)}, u32[]{:S(2)}, u32[]{:S(2)}) async-start(bf16[1,16,128,128]{2,3,0,1:T(8,128)(2,1)} %fusion.2), calls=%async_computation | async-start | bytes 1048576 | tf_op jit(solution)/shard_map/all_to_all | solution.py:59
  256.1 5.4 %copy-start.3 = (bf16[16,128,128]{2,1,0:T(8,128)(2,1)S(1)}, bf16[16,128,128]{2,1,0:T(8,128)(2,1)}, u32[]{:S(2)}) copy-start(bf16[16,128,128]{2,1,0:T(8,128)(2,1)} %gather_fusion.16) | copy-start | bytes 1572868
  256.1 6.9 %copy-start.4 = (bf16[16,128,128]{2,1,0:T(8,128)(2,1)S(1)}, bf16[16,128,128]{2,1,0:T(8,128)(2,1)}, u32[]{:S(2)}) copy-start(bf16[16,128,128]{2,1,0:T(8,128)(2,1)} %gather_fusion.18) | copy-start | bytes 1572868
  261.4 3.1 copy-start
  261.4 3.1 copy-start.5
  261.4 3.4 copy-start.6
  262.9 2.2 copy-start.7
  264.5 1.1 copy-start.8
  264.8 1.1 copy-start.9
  272.9 23.5 %all-to-all-start.2 = ((bf16[32,2,4096]{2,1,0:T(2,128)(2,1)}), bf16[32,2,4096]{2,1,0:T(2,128)(2,1)S(1)}, u32[]{:S(2)}, u32[]{:S(2)}) async-start(bf16[32,2,4096]{2,1,0:T(2,128)(2,1)} %reshape.405), calls=%async_computation.2 | async-start | bytes 1048576 | tf_op jit(solution)/shard_map/all_to_all | solution.py:62
  296.4 20.3 %all-to-all-start.1 = ((bf16[32,2,4096]{2,1,0:T(2,128)(2,1)}), bf16[32,2,4096]{2,1,0:T(2,128)(2,1)S(1)}, u32[]{:S(2)}, u32[]{:S(2)}) async-start(bf16[32,2,4096]{2,1,0:T(2,128)(2,1)} %reshape.407), calls=%async_computation.1 | async-start | bytes 1048576 | tf_op jit(solution)/shard_map/all_to_all | solution.py:61
Sparse Core Ops, SparseCore 0:
  11.5 124.5 all-gather.2
  140.3 115.6 all-gather.4
where the time goes:
time: 428 us; the launch traced here: 427 us
  waiting for transfers between devices  207 us (48%)
  blocking collectives  98.2 us (23%)
  local copies, waits for them, and re-layouts  66.5 us (16%)
  starting transfers between devices  18.1 us (4%)
  between operations  13.9 us (3%)
  matrix products  12.2 us (3%)
  other arithmetic  10.9 us (3%)
    all_gather x1, waiting for transfers between devices, body(): lax.all_gather(occupied_tiles, ('grp', 'blk'), axis=0, tiled=True)  102 us
    psum x1, blocking collectives, body(): total = lax.psum(partial_sum, ('grp', 'blk'))  98.2 us
    all_gather x1, waiting for transfers between devices, body(): lax.all_gather(virtual_tiles, ('grp', 'blk'), axis=0, tiled=True)  81.7 us
    gather x8, local copies, waits for them, and re-layouts, body(): occupied_pick = occupied_all[source_rows[:, slot], slot]  25.8 us
    all_to_all x1, waiting for transfers between devices, body(): lax.all_to_all(occupied_moved, 'blk', split_axis=2, concat_axis=0, tiled=...  11.3 us
    all_to_all x1, waiting for transfers between devices, body(): lax.all_to_all(virtual_part, 'blk', split_axis=2, concat_axis=0, tiled=True)  10.8 us
    gather x8, local copies, waits for them, and re-layouts, body(): occupied_inputs = masked[:, source_rows[:, slot]]  10.6 us
    gather x8, local copies, waits for them, and re-layouts, body(): virtual_inputs = masked[:, partner_rows[:, slot]]  10.6 us
  transfers between devices with their start and end apart: 5, of which 4 were waited for; matrix products, arithmetic and copies ran while one was open for 20% of the time, Pallas kernels for 0%

commit v1 on v0

--- a/solution.py
+++ b/solution.py
@@ -66,7 +66,7 @@
     partial_sum = jnp.einsum(
         "pe,qe->pq", left_side, right_side, preferred_element_type=jnp.float32
     ) * (1.0 / basis_size)
-    total = lax.psum(partial_sum, ("grp", "blk"))
+    total = lax.psum(lax.psum(partial_sum, "blk"), "grp")
     return lax.dynamic_slice_in_dim(total, lax.axis_index("blk") * aux_local, aux_local, 0)
 
 

time: 428 us -> 514 us (1.20)
  blocking collectives: 98.2 us -> 184 us
    psum x1 -> x2, blocking collectives: 98.2 us -> 184 us  [body(): total = lax.psum(lax.psum(partial_sum, 'blk'), 'grp')]
  transfers between devices with their start and end apart: 5 -> 5, of which waited for: 4 -> 4; matrix products, arithmetic and copies ran while one was open for 20% -> 16% of each run, Pallas kernels for 0% -> 0%
where the time goes in v1:
time: 514 us; the launch traced here: 513 us
  waiting for transfers between devices  207 us (40%)
  blocking collectives  184 us (36%)
  local copies, waits for them, and re-layouts  66.6 us (13%)
  starting transfers between devices  18.1 us (4%)
  between operations  13.9 us (3%)
  matrix products  12.2 us (2%)
  other arithmetic  10.9 us (2%)
    psum x2, blocking collectives, body(): total = lax.psum(lax.psum(partial_sum, 'blk'), 'grp')  184 us
    all_gather x1, waiting for transfers between devices, body(): lax.all_gather(occupied_tiles, ('grp', 'blk'), axis=0, tiled=True)  102 us
    all_gather x1, waiting for transfers between devices, body(): lax.all_gather(virtual_tiles, ('grp', 'blk'), axis=0, tiled=True)  81.7 us
    gather x8, local copies, waits for them, and re-layouts, body(): occupied_pick = occupied_all[source_rows[:, slot], slot]  25.8 us
    all_to_all x1, waiting for transfers between devices, body(): lax.all_to_all(occupied_moved, 'blk', split_axis=2, concat_axis=0, tiled=...  11.3 us
    all_to_all x1, waiting for transfers between devices, body(): lax.all_to_all(virtual_part, 'blk', split_axis=2, concat_axis=0, tiled=True)  10.8 us
    gather x8, local copies, waits for them, and re-layouts, body(): occupied_inputs = masked[:, source_rows[:, slot]]  10.6 us
    gather x8, local copies, waits for them, and re-layouts, body(): virtual_inputs = masked[:, partner_rows[:, slot]]  10.6 us
  transfers between devices with their start and end apart: 5, of which 4 were waited for; matrix products, arithmetic and copies ran while one was open for 16% of the time, Pallas kernels for 0%

profile of v1, /device:TPU:1, one launch (start us, length us, event | category | flops | bytes accessed | tf_op | source)
XLA Modules:
  0.0 513.2 jit_solution(9807429323073132744)
XLA Ops:
  34.0 102.1 %all-gather.3.cloned.1.call-done = bf16[16384,128]{1,0:T(8,128)(2,1)} async-done(((bf16[32,128]{1,0:T(8,128)(2,1)}), bf16[16384,128]{1,0:T(8,128)(2,1)}) %all-gather.3.cloned.1.call-update) | async-done | bytes 4194320 | tf_op jit(solution)/shard_map/all_gather | solution.py:32
  136.1 3.6 gather_fusion.1
  139.7 3.6 gather_fusion.3
  143.3 3.6 gather_fusion.5
  147.0 3.6 gather_fusion.7
  150.6 2.9 gather_fusion.9
  153.4 2.8 gather_fusion.11
  156.3 2.8 gather_fusion.13
  159.1 2.8 gather_fusion.15
  162.0 1.7 fusion.25
  163.7 1.6 convolution_add_fusion.13
  168.4 6.0 %all-to-all-start = ((bf16[1,16,128,128]{2,3,0,1:T(8,128)(2,1)}), bf16[1,16,128,128]{2,3,0,1:T(8,128)(2,1)S(1)}, u32[]{:S(2)}, u32[]{:S(2)}) async-start(bf16[1,16,128,128]{2,3,0,1:T(8,128)(2,1)} %fusion.2), calls=%async_computation | async-start | bytes 1048576 | tf_op jit(solution)/shard_map/all_to_all | solution.py:59
  174.4 81.7 %all-gather.5.cloned.1.call-done = bf16[16384,128]{1,0:T(8,128)(2,1)} async-done(((bf16[32,128]{1,0:T(8,128)(2,1)}), bf16[16384,128]{1,0:T(8,128)(2,1)}) %all-gather.5.cloned.1.call-update) | async-done | bytes 4194320 | tf_op jit(solution)/shard_map/all_gather | solution.py:33
  256.1 5.3 %gather_fusion.17 = bf16[16,8,128,128]{3,2,1,0:T(8,128)(2,1)} fusion(bf16[16,8,128,128]{3,2,1,0:T(8,128)(2,1)} %bitcast.152, s32[1024]{0:T(1024)S(1)} %pad_clamp_fusion.8), kind=kCustom, calls=%fused_computation.17 | custom fusion | bytes 8388672 | tf_op jit(solution)/shard_map/gather | solution.py:39
  268.0 3.7 reduce.6
  273.0 6.9 %all-to-all-start.2 = ((bf16[32,2,4096]{2,1,0:T(2,128)(2,1)}), bf16[32,2,4096]{2,1,0:T(2,128)(2,1)S(1)}, u32[]{:S(2)}, u32[]{:S(2)}) async-start(bf16[32,2,4096]{2,1,0:T(2,128)(2,1)} %reshape.405), calls=%async_computation.2 | async-start | bytes 1048576 | tf_op jit(solution)/shard_map/all_to_all | solution.py:62
  280.8 3.7 reduce.7
  285.7 10.8 %all-to-all-done.2 = bf16[32,2,4096]{2,1,0:T(2,128)(2,1)S(1)} async-done(((bf16[32,2,4096]{2,1,0:T(2,128)(2,1)}), bf16[32,2,4096]{2,1,0:T(2,128)(2,1)S(1)}, u32[]{:S(2)}, u32[]{:S(2)}) %all-to-all-start.2) | async-done | bytes 524320 | tf_op jit(solution)/shard_map/all_to_all | solution.py:62
  296.5 5.2 %all-to-all-start.1 = ((bf16[32,2,4096]{2,1,0:T(2,128)(2,1)}), bf16[32,2,4096]{2,1,0:T(2,128)(2,1)S(1)}, u32[]{:S(2)}, u32[]{:S(2)}) async-start(bf16[32,2,4096]{2,1,0:T(2,128)(2,1)} %reshape.407), calls=%async_computation.1 | async-start | bytes 1048576 | tf_op jit(solution)/shard_map/all_to_all | solution.py:61
  302.2 3.0 bitcast_reduce_fusion.1
  305.4 11.3 %all-to-all-done.1 = bf16[32,2,4096]{2,1,0:T(2,128)(2,1)S(1)} async-done(((bf16[32,2,4096]{2,1,0:T(2,128)(2,1)}), bf16[32,2,4096]{2,1,0:T(2,128)(2,1)S(1)}, u32[]{:S(2)}, u32[]{:S(2)}) %all-to-all-start.1) | async-done | bytes 524320 | tf_op jit(solution)/shard_map/all_to_all | solution.py:61
  317.2 3.0 bitcast_reduce_fusion
  321.6 111.0 %psum.14 = f32[32,32]{1,0:T(8,128)S(1)} all-reduce(f32[32,32]{1,0:T(8,128)S(1)} %fusion.3), channel_id=1, replica_groups=mesh['grp'=16,'blk'=32] {'blk'}, use_global_device_ids=true, to_apply=%region_1.2 | all-reduce | flops 1024 | bytes 8192 | tf_op jit(solution)/shard_map/psum | solution.py:69
  432.7 73.2 %psum.15 = f32[32,32]{1,0:T(8,128)S(1)} all-reduce(f32[32,32]{1,0:T(8,128)S(1)} %psum.14), channel_id=1, replica_groups=mesh['grp'=16,'blk'=32] {'grp'}, use_global_device_ids=true, to_apply=%region_2.3 | all-reduce | flops 1024 | bytes 8192 | tf_op jit(solution)/shard_map/psum | solution.py:69
  (96 shorter events, 43.3 us)
Async XLA Ops:
  6.5 129.6 %all-gather.3.cloned.1.call-start = ((), (), s32[]{:S(2)}) async-start(), calls=%async_computation.3 | async-start | bytes 4202496 | tf_op jit(solution)/shard_map/all_gather | solution.py:32
  7.3 248.8 %all-gather.5.cloned.1.call-start = ((), (), s32[]{:S(2)}) async-start(), calls=%async_computation.4 | async-start | bytes 4202496 | tf_op jit(solution)/shard_map/all_gather | solution.py:33
  23.3 10.7 %copy-start.15 = (s32[16]{0:T(128)S(1)}, s32[16]{0:T(128)}, u32[]{:S(2)}) copy-start(s32[16]{0:T(128)} %param.9) | copy-start | bytes 196
  162.0 3.4 copy-start.2
  162.0 3.4 copy-start.11
  162.0 3.7 copy-start.1
  162.0 3.7 copy-start.10
  163.7 2.4 copy-start.13
  165.4 1.1 copy-start.12
  165.8 1.1 copy-start.14
  168.4 104.6 %all-to-all-start = ((bf16[1,16,128,128]{2,3,0,1:T(8,128)(2,1)}), bf16[1,16,128,128]{2,3,0,1:T(8,128)(2,1)S(1)}, u32[]{:S(2)}, u32[]{:S(2)}) async-start(bf16[1,16,128,128]{2,3,0,1:T(8,128)(2,1)} %fusion.2), calls=%async_computation | async-start | bytes 1048576 | tf_op jit(solution)/shard_map/all_to_all | solution.py:59
  256.1 5.4 %copy-start.3 = (bf16[16,128,128]{2,1,0:T(8,128)(2,1)S(1)}, bf16[16,128,128]{2,1,0:T(8,128)(2,1)}, u32[]{:S(2)}) copy-start(bf16[16,128,128]{2,1,0:T(8,128)(2,1)} %gather_fusion.16) | copy-start | bytes 1572868
  256.1 6.9 %copy-start.4 = (bf16[16,128,128]{2,1,0:T(8,128)(2,1)S(1)}, bf16[16,128,128]{2,1,0:T(8,128)(2,1)}, u32[]{:S(2)}) copy-start(bf16[16,128,128]{2,1,0:T(8,128)(2,1)} %gather_fusion.18) | copy-start | bytes 1572868
  261.5 3.1 copy-start
  261.5 3.1 copy-start.5
  261.5 3.4 copy-start.6
  263.0 2.2 copy-start.7
  264.6 1.1 copy-start.8
  264.9 1.1 copy-start.9
  273.0 23.5 %all-to-all-start.2 = ((bf16[32,2,4096]{2,1,0:T(2,128)(2,1)}), bf16[32,2,4096]{2,1,0:T(2,128)(2,1)S(1)}, u32[]{:S(2)}, u32[]{:S(2)}) async-start(bf16[32,2,4096]{2,1,0:T(2,128)(2,1)} %reshape.405), calls=%async_computation.2 | async-start | bytes 1048576 | tf_op jit(solution)/shard_map/all_to_all | solution.py:62
  296.5 20.3 %all-to-all-start.1 = ((bf16[32,2,4096]{2,1,0:T(2,128)(2,1)}), bf16[32,2,4096]{2,1,0:T(2,128)(2,1)S(1)}, u32[]{:S(2)}, u32[]{:S(2)}) async-start(bf16[32,2,4096]{2,1,0:T(2,128)(2,1)} %reshape.407), calls=%async_computation.1 | async-start | bytes 1048576 | tf_op jit(solution)/shard_map/all_to_all | solution.py:61
Sparse Core Ops, SparseCore 0:
  11.5 124.5 all-gather.2
  140.3 115.7 all-gather.4
